TPU v7x, 32 devices: a whole 2x2x4 slice. The times are simulated.
32 devices in a mesh: grp: 2 (over x), dev: 16 (over z, y, core).
Axes of the slice: x: 2, y: 2, z: 4, core: 2. Of those that a mesh axis runs over, the one named last changes fastest.
Arguments:
- query: bfloat16 [64, 64, 128], P(('grp', 'dev')), may hold values from -6 to 6
- key_cache: bfloat16 [64, 512, 8, 128], P(('grp', 'dev')), may hold values from -6 to 6
- value_cache: bfloat16 [64, 512, 8, 128], P(('grp', 'dev')), may hold values from -6 to 6
- lengths: int32 [64], P(('grp', 'dev')), may hold values from 1 to 512, 16384 in all
- out_weight: bfloat16 [8192, 8192], P('dev', 'grp'), may hold values from -0.0625 to 0.0625
- resid: bfloat16 [64, 8192], P('dev', 'grp'), may hold values from -6 to 6
- norm_gain: bfloat16 [8192], P('grp'), may hold values from 0.5 to 1.5
- gate_weight: bfloat16 [8192, 28672], P('grp', 'dev'), may hold values from -0.0625 to 0.0625
- up_weight: bfloat16 [8192, 28672], P('grp', 'dev'), may hold values from -0.0625 to 0.0625
- down_weight: bfloat16 [28672, 8192], P('dev', 'grp'), may hold values from -0.03125 to 0.03125
Outputs:
- layer_out: bfloat16 [64, 8192], P('dev', 'grp')
Inputs may be any that keep to these rules, and one draw needn't show every extreme that they name: `lengths`: some request has exactly 512 live slots.
All inputs are finite; a program needn't handle non-finite values. No bound on the sum of `lengths` on one device may be relied on, other than what follows from the above.
Results may differ from a plain program's by a relative error of at most 0.015.
Values may be sent and summed in bfloat16 or wider, within the bound.
A program may use at most 128 MiB of HBM per device.

v0:
```python
import jax
import jax.numpy as jnp
from jax import lax
from jax.sharding import PartitionSpec as P


def attend(query, key_cache, value_cache, lengths):
    rows, heads, width = query.shape
    kv_heads = key_cache.shape[2]
    group = heads // kv_heads
    grouped = query.reshape(rows, kv_heads, group, width)
    scores = jnp.einsum(
        "rhgd,rlhd->rhgl", grouped, key_cache, preferred_element_type=jnp.float32
    ) * width ** (-0.5)
    places = jnp.arange(key_cache.shape[1], dtype=jnp.int32)
    valid = places[None, :] < lengths[:, None]
    scores = jnp.where(valid[:, None, None, :], scores, -1e30)
    top = jnp.max(scores, axis=-1, keepdims=True)
    weights = jnp.exp(scores - top)
    probs = (weights / jnp.sum(weights, axis=-1, keepdims=True)).astype(jnp.bfloat16)
    mixed = jnp.einsum("rhgl,rlhd->rhgd", probs, value_cache, preferred_element_type=jnp.float32)
    return mixed.reshape(rows, heads * width).astype(jnp.bfloat16)


def per_device(
    query,
    key_cache,
    value_cache,
    lengths,
    out_weight,
    resid,
    norm_gain,
    gate_weight,
    up_weight,
    down_weight,
):
    attn = attend(query, key_cache, value_cache, lengths)
    block_cols = out_weight.shape[0]
    first_col = lax.axis_index("dev") * block_cols
    cols = lax.dynamic_slice_in_dim(
        lax.all_gather(attn, ("grp", "dev"), axis=0, tiled=True), first_col, block_cols, 1
    )
    proj_terms = jnp.dot(cols, out_weight, preferred_element_type=jnp.float32)
    x = resid.astype(jnp.float32) + lax.psum_scatter(
        proj_terms, "dev", scatter_dimension=0, tiled=True
    )
    width_all = x.shape[1] * lax.axis_size("grp")
    sumsq = lax.psum(jnp.sum(x * x, axis=1), "grp")
    normed = (
        x * lax.rsqrt(sumsq / width_all + 1e-05)[:, None] * norm_gain.astype(jnp.float32)
    ).astype(jnp.bfloat16)
    piece = lax.all_gather(normed, "dev", axis=0, tiled=True)
    half_terms = jnp.concatenate(
        [
            jnp.dot(piece, gate_weight, preferred_element_type=jnp.float32),
            jnp.dot(piece, up_weight, preferred_element_type=jnp.float32),
        ],
        axis=1,
    )
    both = lax.psum(half_terms.astype(jnp.bfloat16), "grp").astype(jnp.float32)
    hidden_cols = gate_weight.shape[1]
    gate = both[:, :hidden_cols]
    up = both[:, hidden_cols:]
    hidden = (jax.nn.silu(gate) * up).astype(jnp.bfloat16)
    ffn_rows = lax.psum_scatter(
        jnp.dot(hidden, down_weight, preferred_element_type=jnp.float32),
        "dev",
        scatter_dimension=0,
        tiled=True,
    )
    return (x + ffn_rows).astype(jnp.bfloat16)


def solution(mesh):
    placed = (
        P(("grp", "dev"), None, None),
        P(("grp", "dev"), None, None, None),
        P(("grp", "dev"), None, None, None),
        P(("grp", "dev")),
        P("dev", "grp"),
        P("dev", "grp"),
        P("grp"),
        P("grp", "dev"),
        P("grp", "dev"),
        P("dev", "grp"),
    )
    return jax.shard_map(
        per_device, mesh=mesh, in_specs=placed, out_specs=P("dev", "grp"), check_vma=False
    )
```

profile of v0, /device:TPU:0, one launch (start us, length us, event | category | flops | bytes accessed | tf_op | source)
XLA Modules:
  0.0 347.9 jit_solution(15746743131024164946)
XLA Ops:
  6.5 0.0 copy-start
  6.5 0.0 all-gather.4.cloned.1.call-start
  6.5 0.9 iota_compare_fusion
  7.4 0.7 copy-done
  8.1 1.4 fusion.10
  9.6 0.2 fusion.28
  9.8 2.1 fusion.13
  11.9 0.6 reshape.27
  12.5 0.0 all-gather.4.cloned.1.call-update
  12.6 0.0 all-reduce.8.cloned.1.call-start
  12.6 0.0 copy-start.3
  12.6 0.0 copy-start.1
  12.6 0.0 copy-start.2
  12.7 56.5 %all-gather.4.cloned.1.call-done = bf16[32,2,8192]{2,1,0:T(2,128)(2,1)} async-done(((bf16[1,2,8192]{2,1,0:T(2,128)(2,1)}), bf16[32,2,8192]{2,1,0:T(2,128)(2,1)}) %all-gather.4.cloned.1.call-update) | async-done | bytes 1048592 | tf_op jit(solution)/shard_map/all_gather | solution.py:41
  69.1 1.5 reshape.28
  70.6 4.1 %fusion.22 = f32[64,4096]{1,0:T(8,128)} fusion(bf16[512,4096]{1,0:T(8,128)(2,1)} %param.14, bf16[64,8192]{1,0:T(8,128)(2,1)S(1)} %reshape.28, s32[]{:T(128)S(6)} %select_n.8), kind=kOutput, calls=%fused_computation.24 | convolution fusion | flops 268435456 | bytes 5308420 | tf_op jit(solution)/shard_map/dot_general | solution.py:43
  74.7 0.0 all-reduce.8.cloned.1.call-update
  74.7 0.0 all-reduce.6.cloned.1.call-start
  74.8 0.0 copy-done.3
  74.8 0.6 dynamic-slice
  76.0 91.0 %all-reduce.8.cloned.1.call-done = f32[64,4096]{1,0:T(8,128)} async-done(((f32[64,4096]{1,0:T(8,128)}), f32[64,4096]{1,0:T(8,128)}) %all-reduce.8.cloned.1.call-update) | async-done | bytes 1048592
  167.0 0.0 copy-done.1
  167.0 1.1 multiply_reduce_fusion
  168.0 0.0 copy-done.2
  168.1 4.9 %psum.14 = f32[4]{0:T(128)S(1)} all-reduce(f32[4]{0:T(128)S(1)} %multiply_reduce_fusion), channel_id=1, replica_groups=mesh['grp'=2,'dev'=16] {'grp'}, use_global_device_ids=true, to_apply=%region_4.5 | all-reduce | flops 4 | bytes 32 | tf_op jit(solution)/shard_map/psum | solution.py:48
  173.0 1.0 fusion.24
  174.0 21.1 %all-gather.1 = bf16[16,4,4096]{2,1,0:T(4,128)(2,1)S(1)} all-gather(bf16[1,4,4096]{2,1,0:T(4,128)(2,1)S(1)} %fusion.24), channel_id=1, replica_groups=mesh['grp'=2,'dev'=16] {'dev'}, dimensions={0}, use_global_device_ids=true | all-gather | bytes 557056 | tf_op jit(solution)/shard_map/all_gather | solution.py:52
  195.1 0.1 reshape.30
  195.2 7.8 %convolution_convert_fusion = bf16[64,1792]{1,0:T(8,128)(2,1)S(1)} fusion(bf16[64,4096]{1,0:T(8,128)(2,1)S(1)} %reshape.30, bf16[4096,1792]{1,0:T(8,128)(2,1)} %param.18), kind=kOutput, calls=%fused_computation.1 | convolution fusion | flops 939638784 | bytes 15433728 | tf_op jit(solution)/shard_map/dot_general | solution.py:56
  203.0 7.8 %convolution_convert_fusion.1 = bf16[64,1792]{1,0:T(8,128)(2,1)S(1)} fusion(bf16[64,4096]{1,0:T(8,128)(2,1)S(1)} %reshape.30, bf16[4096,1792]{1,0:T(8,128)(2,1)} %param.17), kind=kOutput, calls=%fused_computation.2 | convolution fusion | flops 939638784 | bytes 15433728 | tf_op jit(solution)/shard_map/dot_general | solution.py:55
  210.8 0.8 pad_maximum_fusion
  211.6 0.0 all-reduce.6.cloned.1.call-update
  211.7 0.0 all-reduce.10.cloned.1.call-start
  211.7 24.5 %all-reduce.6.cloned.1.call-done = bf16[64,3584]{1,0:T(8,128)(2,1)} async-done(((bf16[64,3584]{1,0:T(8,128)(2,1)}), bf16[64,3584]{1,0:T(8,128)(2,1)}) %all-reduce.6.cloned.1.call-update) | async-done | bytes 458768 | tf_op jit(solution)/shard_map/psum | solution.py:60
  236.3 1.1 convert_element_type.34
  237.3 8.8 %fusion.17 = f32[64,4096]{1,0:T(8,128)} fusion(bf16[1792,4096]{1,0:T(8,128)(2,1)} %param.19, f32[64,3584]{1,0:T(8,128)S(1)} %convert_element_type.34), kind=kOutput, calls=%fused_computation.16 | convolution fusion | flops 940212224 | bytes 16646144 | tf_op jit(solution)/shard_map/dot_general | solution.py:66
  246.2 0.0 all-reduce.10.cloned.1.call-update
  246.2 93.5 %all-reduce.10.cloned.1.call-done = f32[64,4096]{1,0:T(8,128)} async-done(((f32[64,4096]{1,0:T(8,128)}), f32[64,4096]{1,0:T(8,128)}) %all-reduce.10.cloned.1.call-update) | async-done | bytes 1048592
  339.7 1.6 fusion.21
  (2 shorter events, 0.0 us)
Async XLA Ops:
  6.5 1.6 copy-start
  6.5 62.6 %all-gather.4.cloned.1.call-start = ((), (), s32[]{:S(2)}) async-start(), calls=%async_computation.1 | async-start | bytes 1081344 | tf_op jit(solution)/shard_map/all_gather | solution.py:41
  12.6 154.4 %all-reduce.8.cloned.1.call-start = ((), (), s32[]{:S(2)}) async-start(), calls=%async_computation.2 | async-start | bytes 2097152
  12.6 62.1 %copy-start.3 = (u32[32]{0:T(128)S(1)}, u32[32]{0:T(128)}, u32[]{:S(2)}) copy-start(u32[32]{0:T(128)} %constant.33) | copy-start | bytes 388
  12.6 154.4 %copy-start.1 = (bf16[4,4096]{1,0:T(4,128)(2,1)S(1)}, bf16[4,4096]{1,0:T(4,128)(2,1)}, u32[]{:S(2)}) copy-start(bf16[4,4096]{1,0:T(4,128)(2,1)} %param.15) | copy-start | bytes 98308
  12.6 155.4 %copy-start.2 = (bf16[4096]{0:T(1024)(128)(2,1)S(1)}, bf16[4096]{0:T(1024)(128)(2,1)}, u32[]{:S(2)}) copy-start(bf16[4096]{0:T(1024)(128)(2,1)} %param.16) | copy-start | bytes 24580
  74.7 161.6 %all-reduce.6.cloned.1.call-start = ((), (), s32[]{:S(2)}) async-start(), calls=%async_computation | async-start | bytes 917504 | tf_op jit(solution)/shard_map/psum | solution.py:60
  211.7 128.1 %all-reduce.10.cloned.1.call-start = ((), (), s32[]{:S(2)}) async-start(), calls=%async_computation.3 | async-start | bytes 2097152
Sparse Core Ops, SparseCore 0:
  12.7 56.4 all-gather.3
  74.8 92.1 all-reduce.7
  211.8 24.4 all-reduce.5
  246.3 93.3 all-reduce.9
where the time goes:
time: 348 us
  waiting for transfers between devices  266 us (76%)
  matrix products  32.1 us (9%)
  blocking collectives  26 us (7%)
  between operations  13.9 us (4%)
  other arithmetic  6.65 us (2%)
  local copies, waits for them, and re-layouts  3.56 us (1%)
    unnamed x6, waiting for transfers between devices  185 us
    all_gather x1, waiting for transfers between devices, per_device(): lax.all_gather(attn, ('grp', 'dev'), axis=0, tiled=True)  56.5 us
    psum x1, waiting for transfers between devices, per_device(): both = lax.psum(half_terms.astype(jnp.bfloat16), 'grp').astype(jnp.float32)  24.5 us
    all_gather x1, blocking collectives, per_device(): piece = lax.all_gather(normed, 'dev', axis=0, tiled=True)  21.1 us
    dot_general x1, matrix products, per_device(): jnp.dot(hidden, down_weight, preferred_element_type=jnp.float32)  8.84 us
    dot_general x1, matrix products, per_device(): jnp.dot(piece, up_weight, preferred_element_type=jnp.float32)  7.81 us
    dot_general x1, matrix products, per_device(): jnp.dot(piece, gate_weight, preferred_element_type=jnp.float32)  7.81 us
  transfers between devices with their start and end apart: 4, of which 4 were waited for; matrix products, arithmetic and copies ran while one was open for 0% of the time, Pallas kernels for 0%

commit v1 on v0

--- a/solution.py
+++ b/solution.py
@@ -2,6 +2,34 @@
 import jax.numpy as jnp
 from jax import lax
 from jax.sharding import PartitionSpec as P
+
+
+def _review_clusters(z, pos_dim):
+    p_next = list(z.shape[1:])
+    p_next[pos_dim] *= z.shape[0]
+    return jnp.moveaxis(z, 0, pos_dim).reshape(p_next)
+
+
+def compute_the_groups(payload, peer_axis, along_dim=0):
+    n_parts = lax.axis_size(peer_axis)
+    so_far_all = tuple(((jj, (jj + 1) % n_parts) for jj in range(n_parts)))
+    nodes = tuple(((kk, j) for j, kk in so_far_all))
+    f_next, seen_now = ([], [])
+    for dev_j in range(n_parts - 1):
+        if dev_j % 2 == 0:
+            f_next.append(
+                lax.ppermute(
+                    f_next[-1] if f_next else payload, axis_name=peer_axis, perm=so_far_all
+                )
+            )
+        else:
+            seen_now.append(
+                lax.ppermute(seen_now[-1] if seen_now else payload, axis_name=peer_axis, perm=nodes)
+            )
+    last = jnp.stack([*f_next[::-1], payload, *seen_now], axis=0)
+    n_now = lax.axis_index(peer_axis) - len(f_next)
+    last = last[(jnp.arange(n_parts) - n_now) % n_parts]
+    return _review_clusters(last, along_dim)
 
 
 def attend(query, key_cache, value_cache, lengths):
@@ -49,7 +77,7 @@
     normed = (
         x * lax.rsqrt(sumsq / width_all + 1e-05)[:, None] * norm_gain.astype(jnp.float32)
     ).astype(jnp.bfloat16)
-    piece = lax.all_gather(normed, "dev", axis=0, tiled=True)
+    piece = compute_the_groups(normed, "dev")
     half_terms = jnp.concatenate(
         [
             jnp.dot(piece, gate_weight, preferred_element_type=jnp.float32),

time: 348 us -> 381 us (1.095)
  starting transfers between devices: 0.13 us -> 31.3 us
  blocking collectives: 26 us -> 4.94 us
  waiting for transfers between devices: 266 us -> 286 us
    ppermute x0 -> x15, starting transfers between devices: none -> 31.2 us  [the longest x7 31.1 us: compute_the_groups(): lax.ppermute(seen_now[-1] if seen_now else payload, axis_name=peer_axis,...]
    all_gather x1 -> x0, blocking collectives: 21.1 us -> none  [per_device(): piece = lax.all_gather(normed, 'dev', axis=0, tiled=True)]
    ppermute x0 -> x15, waiting for transfers between devices: none -> 17.1 us  [the longest x8 17 us: compute_the_groups(): lax.ppermute(f_next[-1] if f_next else payload, axis_name=peer_axis, perm...]
  transfers between devices with their start and end apart: 4 -> 19, of which waited for: 4 -> 13; matrix products, arithmetic and copies ran while one was open for 0% -> 0% of each run, Pallas kernels for 0% -> 0%
where the time goes in v1:
time: 381 us; the launch traced here: 380 us
  waiting for transfers between devices  286 us (75%)
  matrix products  32.1 us (8%)
  starting transfers between devices  31.3 us (8%)
  between operations  14 us (4%)
  other arithmetic  6.69 us (2%)
  blocking collectives  4.94 us (1%)
  local copies, waits for them, and re-layouts  4.93 us (1%)
    unnamed x6, waiting for transfers between devices  185 us
    all_gather x1, waiting for transfers between devices, per_device(): lax.all_gather(attn, ('grp', 'dev'), axis=0, tiled=True)  56.6 us
    ppermute x7, starting transfers between devices, compute_the_groups(): lax.ppermute(seen_now[-1] if seen_now else payload, axis_name=peer_axis,...  31.1 us
    psum x1, waiting for transfers between devices, per_device(): both = lax.psum(half_terms.astype(jnp.bfloat16), 'grp').astype(jnp.float32)  28.1 us
    ppermute x8, waiting for transfers between devices, compute_the_groups(): lax.ppermute(f_next[-1] if f_next else payload, axis_name=peer_axis, perm...  17 us
    dot_general x1, matrix products, per_device(): jnp.dot(hidden, down_weight, preferred_element_type=jnp.float32)  8.85 us
    dot_general x1, matrix products, per_device(): jnp.dot(piece, up_weight, preferred_element_type=jnp.float32)  7.81 us
    dot_general x1, matrix products, per_device(): jnp.dot(piece, gate_weight, preferred_element_type=jnp.float32)  7.8 us
  transfers between devices with their start and end apart: 19, of which 13 were waited for; matrix products, arithmetic and copies ran while one was open for 0% of the time, Pallas kernels for 0%

profile of v1, /device:TPU:0, one launch (start us, length us, event | category | flops | bytes accessed | tf_op | source)
XLA Modules:
  0.0 380.3 jit_solution(3090173944395670997)
XLA Ops:
  6.5 0.9 iota_compare_fusion
  7.4 0.7 copy-done
  8.1 1.4 fusion.10
  9.6 0.2 fusion.29
  9.8 2.1 fusion.13
  11.9 0.6 reshape.88
  12.5 0.0 all-gather.3.cloned.1.call-update
  12.6 0.0 all-reduce.8.cloned.1.call-start
  12.7 56.6 %all-gather.3.cloned.1.call-done = bf16[32,2,8192]{2,1,0:T(2,128)(2,1)} async-done(((bf16[1,2,8192]{2,1,0:T(2,128)(2,1)}), bf16[32,2,8192]{2,1,0:T(2,128)(2,1)}) %all-gather.3.cloned.1.call-update) | async-done | bytes 1048592 | tf_op jit(solution)/shard_map/all_gather | solution.py:69
  69.2 1.5 reshape.89
  70.7 4.1 %fusion.22 = f32[64,4096]{1,0:T(8,128)} fusion(bf16[512,4096]{1,0:T(8,128)(2,1)} %param.14, bf16[64,8192]{1,0:T(8,128)(2,1)S(1)} %reshape.89, s32[]{:T(128)S(6)} %select_n.32), kind=kOutput, calls=%fused_computation.25 | convolution fusion | flops 268435456 | bytes 5308420 | tf_op jit(solution)/shard_map/dot_general | solution.py:71
  74.8 0.0 all-reduce.8.cloned.1.call-update
  74.8 0.0 all-reduce.6.cloned.1.call-start
  74.9 0.6 dynamic-slice
  76.1 91.0 %all-reduce.8.cloned.1.call-done = f32[64,4096]{1,0:T(8,128)} async-done(((f32[64,4096]{1,0:T(8,128)}), f32[64,4096]{1,0:T(8,128)}) %all-reduce.8.cloned.1.call-update) | async-done | bytes 1048592
  167.2 1.1 multiply_reduce_fusion
  168.2 4.9 %psum.14 = f32[4]{0:T(128)S(1)} all-reduce(f32[4]{0:T(128)S(1)} %multiply_reduce_fusion), channel_id=1, replica_groups=mesh['grp'=2,'dev'=16] {'grp'}, use_global_device_ids=true, to_apply=%region_4.5 | all-reduce | flops 4 | bytes 32 | tf_op jit(solution)/shard_map/psum | solution.py:76
  173.2 1.0 multiply_convert_fusion
  174.2 0.1 collective-permute-start
  174.2 6.0 %collective-permute-done = bf16[4,4096]{1,0:T(4,128)(2,1)S(1)} collective-permute-done((bf16[4,4096]{1,0:T(4,128)(2,1)S(1)}, bf16[4,4096]{1,0:T(4,128)(2,1)S(1)}, u32[]{:S(2)}, u32[]{:S(2)}) %collective-permute-start) | collective-permute-done | bytes 32800 | tf_op jit(solution)/shard_map/ppermute | solution.py:21
  180.3 4.4 %collective-permute-start.8 = (bf16[4,4096]{1,0:T(4,128)(2,1)S(1)}, bf16[4,4096]{1,0:T(4,128)(2,1)S(1)}, u32[]{:S(2)}, u32[]{:S(2)}) collective-permute-start(bf16[4,4096]{1,0:T(4,128)(2,1)S(1)} %multiply_convert_fusion), channel_id=1, source_target_pairs={{1,0},{2,1},{3,2},{4,3},{5,4},{6,5},{7,6},{8,7},{9,8},{10,9},{11,1... | collective-permute-start | bytes 98312 | tf_op jit(solution)/shard_map/ppermute | solution.py:27
  184.7 1.6 collective-permute-done.1
  186.3 4.4 %collective-permute-start.9 = (bf16[4,4096]{1,0:T(4,128)(2,1)S(1)}, bf16[4,4096]{1,0:T(4,128)(2,1)S(1)}, u32[]{:S(2)}, u32[]{:S(2)}) collective-permute-start(bf16[4,4096]{1,0:T(4,128)(2,1)S(1)} %collective-permute-done.8), channel_id=1, source_target_pairs={{1,0},{2,1},{3,2},{4,3},{5,4},{6,5},{7,6},{8,7},{9,8},{10,9},{11,1... | collective-permute-start | bytes 98312 | tf_op jit(solution)/shard_map/ppermute | solution.py:27
  190.8 1.6 collective-permute-done.2
  192.3 4.4 %collective-permute-start.10 = (bf16[4,4096]{1,0:T(4,128)(2,1)S(1)}, bf16[4,4096]{1,0:T(4,128)(2,1)S(1)}, u32[]{:S(2)}, u32[]{:S(2)}) collective-permute-start(bf16[4,4096]{1,0:T(4,128)(2,1)S(1)} %collective-permute-done.9), channel_id=1, source_target_pairs={{1,0},{2,1},{3,2},{4,3},{5,4},{6,5},{7,6},{8,7},{9,8},{10,9},{11,1... | collective-permute-start | bytes 98312 | tf_op jit(solution)/shard_map/ppermute | solution.py:27
  196.8 1.6 collective-permute-done.3
  198.4 4.4 %collective-permute-start.11 = (bf16[4,4096]{1,0:T(4,128)(2,1)S(1)}, bf16[4,4096]{1,0:T(4,128)(2,1)S(1)}, u32[]{:S(2)}, u32[]{:S(2)}) collective-permute-start(bf16[4,4096]{1,0:T(4,128)(2,1)S(1)} %collective-permute-done.10), channel_id=1, source_target_pairs={{1,0},{2,1},{3,2},{4,3},{5,4},{6,5},{7,6},{8,7},{9,8},{10,9},{11,1... | collective-permute-start | bytes 98312 | tf_op jit(solution)/shard_map/ppermute | solution.py:27
  202.8 1.6 collective-permute-done.4
  204.4 4.4 %collective-permute-start.12 = (bf16[4,4096]{1,0:T(4,128)(2,1)S(1)}, bf16[4,4096]{1,0:T(4,128)(2,1)S(1)}, u32[]{:S(2)}, u32[]{:S(2)}) collective-permute-start(bf16[4,4096]{1,0:T(4,128)(2,1)S(1)} %collective-permute-done.11), channel_id=1, source_target_pairs={{1,0},{2,1},{3,2},{4,3},{5,4},{6,5},{7,6},{8,7},{9,8},{10,9},{11,1... | collective-permute-start | bytes 98312 | tf_op jit(solution)/shard_map/ppermute | solution.py:27
  208.9 1.6 collective-permute-done.5
  210.5 4.5 %collective-permute-start.13 = (bf16[4,4096]{1,0:T(4,128)(2,1)S(1)}, bf16[4,4096]{1,0:T(4,128)(2,1)S(1)}, u32[]{:S(2)}, u32[]{:S(2)}) collective-permute-start(bf16[4,4096]{1,0:T(4,128)(2,1)S(1)} %collective-permute-done.12), channel_id=1, source_target_pairs={{1,0},{2,1},{3,2},{4,3},{5,4},{6,5},{7,6},{8,7},{9,8},{10,9},{11,1... | collective-permute-start | bytes 98312 | tf_op jit(solution)/shard_map/ppermute | solution.py:27
  215.0 1.5 collective-permute-done.6
  216.5 0.1 collective-permute-done.13
  216.6 4.4 %collective-permute-start.14 = (bf16[4,4096]{1,0:T(4,128)(2,1)S(1)}, bf16[4,4096]{1,0:T(4,128)(2,1)S(1)}, u32[]{:S(2)}, u32[]{:S(2)}) collective-permute-start(bf16[4,4096]{1,0:T(4,128)(2,1)S(1)} %collective-permute-done.13), channel_id=1, source_target_pairs={{1,0},{2,1},{3,2},{4,3},{5,4},{6,5},{7,6},{8,7},{9,8},{10,9},{11,1... | collective-permute-start | bytes 98312 | tf_op jit(solution)/shard_map/ppermute | solution.py:27
  221.0 1.5 collective-permute-done.7
  223.0 1.0 gather_fusion
  224.0 0.1 reshape.79
  224.1 7.8 %convolution_convert_fusion = bf16[64,1792]{1,0:T(8,128)(2,1)S(1)} fusion(bf16[64,4096]{1,0:T(8,128)(2,1)S(1)} %reshape.79, bf16[4096,1792]{1,0:T(8,128)(2,1)} %param.18), kind=kOutput, calls=%fused_computation.2 | convolution fusion | flops 939638784 | bytes 15433728 | tf_op jit(solution)/shard_map/dot_general | solution.py:84
  231.9 7.8 %convolution_convert_fusion.1 = bf16[64,1792]{1,0:T(8,128)(2,1)S(1)} fusion(bf16[64,4096]{1,0:T(8,128)(2,1)S(1)} %reshape.79, bf16[4096,1792]{1,0:T(8,128)(2,1)} %param.17), kind=kOutput, calls=%fused_computation.3 | convolution fusion | flops 939638784 | bytes 15433728 | tf_op jit(solution)/shard_map/dot_general | solution.py:83
  239.7 0.8 pad_maximum_fusion
  240.5 0.0 all-reduce.6.cloned.1.call-update
  240.6 0.0 all-reduce.10.cloned.1.call-start
  240.6 28.1 %all-reduce.6.cloned.1.call-done = bf16[64,3584]{1,0:T(8,128)(2,1)} async-done(((bf16[64,3584]{1,0:T(8,128)(2,1)}), bf16[64,3584]{1,0:T(8,128)(2,1)}) %all-reduce.6.cloned.1.call-update) | async-done | bytes 458768 | tf_op jit(solution)/shard_map/psum | solution.py:88
  268.7 1.1 convert_element_type.34
  269.8 8.8 %fusion.17 = f32[64,4096]{1,0:T(8,128)} fusion(bf16[1792,4096]{1,0:T(8,128)(2,1)} %param.19, f32[64,3584]{1,0:T(8,128)S(1)} %convert_element_type.34), kind=kOutput, calls=%fused_computation.17 | convolution fusion | flops 940212224 | bytes 16646144 | tf_op jit(solution)/shard_map/dot_general | solution.py:94
  278.6 0.0 all-reduce.10.cloned.1.call-update
  278.6 93.5 %all-reduce.10.cloned.1.call-done = f32[64,4096]{1,0:T(8,128)} async-done(((f32[64,4096]{1,0:T(8,128)}), f32[64,4096]{1,0:T(8,128)}) %all-reduce.10.cloned.1.call-update) | async-done | bytes 1048592
  372.1 1.6 fusion.21
  (41 shorter events, 0.5 us)
Async XLA Ops:
  6.5 1.6 copy-start
  6.5 62.7 %all-gather.3.cloned.1.call-start = ((), (), s32[]{:S(2)}) async-start(), calls=%async_computation.1 | async-start | bytes 1081344 | tf_op jit(solution)/shard_map/all_gather | solution.py:69
  12.6 154.6 %all-reduce.8.cloned.1.call-start = ((), (), s32[]{:S(2)}) async-start(), calls=%async_computation.2 | async-start | bytes 2097152
  12.6 62.2 %copy-start.3 = (u32[32]{0:T(128)S(1)}, u32[32]{0:T(128)}, u32[]{:S(2)}) copy-start(u32[32]{0:T(128)} %constant.52) | copy-start | bytes 388
  12.6 154.5 %copy-start.1 = (bf16[4,4096]{1,0:T(4,128)(2,1)S(1)}, bf16[4,4096]{1,0:T(4,128)(2,1)}, u32[]{:S(2)}) copy-start(bf16[4,4096]{1,0:T(4,128)(2,1)} %param.15) | copy-start | bytes 98308
  12.6 155.6 %copy-start.2 = (bf16[4096]{0:T(1024)(128)(2,1)S(1)}, bf16[4096]{0:T(1024)(128)(2,1)}, u32[]{:S(2)}) copy-start(bf16[4096]{0:T(1024)(128)(2,1)} %param.16) | copy-start | bytes 24580
  74.8 193.9 %all-reduce.6.cloned.1.call-start = ((), (), s32[]{:S(2)}) async-start(), calls=%async_computation | async-start | bytes 917504 | tf_op jit(solution)/shard_map/psum | solution.py:88
  174.2 6.1 %collective-permute-start = (bf16[4,4096]{1,0:T(4,128)(2,1)S(1)}, bf16[4,4096]{1,0:T(4,128)(2,1)S(1)}, u32[]{:S(2)}, u32[]{:S(2)}) collective-permute-start(bf16[4,4096]{1,0:T(4,128)(2,1)S(1)} %multiply_convert_fusion), channel_id=1, source_target_pairs={{0,1},{1,2},{2,3},{3,4},{4,5},{5,6},{6,7},{7,8},{8,9},{9,10},{10,1... | collective-permute-start | bytes 98312 | tf_op jit(solution)/shard_map/ppermute | solution.py:21
  180.3 6.0 %collective-permute-start.1 = (bf16[4,4096]{1,0:T(4,128)(2,1)S(1)}, bf16[4,4096]{1,0:T(4,128)(2,1)S(1)}, u32[]{:S(2)}, u32[]{:S(2)}) collective-permute-start(bf16[4,4096]{1,0:T(4,128)(2,1)S(1)} %collective-permute-done), channel_id=1, source_target_pairs={{0,1},{1,2},{2,3},{3,4},{4,5},{5,6},{6,7},{7,8},{8,9},{9,10},{10,1... | collective-permute-start | bytes 98312 | tf_op jit(solution)/shard_map/ppermute | solution.py:21
  180.3 6.0 %collective-permute-start.8 = (bf16[4,4096]{1,0:T(4,128)(2,1)S(1)}, bf16[4,4096]{1,0:T(4,128)(2,1)S(1)}, u32[]{:S(2)}, u32[]{:S(2)}) collective-permute-start(bf16[4,4096]{1,0:T(4,128)(2,1)S(1)} %multiply_convert_fusion), channel_id=1, source_target_pairs={{1,0},{2,1},{3,2},{4,3},{5,4},{6,5},{7,6},{8,7},{9,8},{10,9},{11,1... | collective-permute-start | bytes 98312 | tf_op jit(solution)/shard_map/ppermute | solution.py:27
  186.3 6.0 %collective-permute-start.2 = (bf16[4,4096]{1,0:T(4,128)(2,1)S(1)}, bf16[4,4096]{1,0:T(4,128)(2,1)S(1)}, u32[]{:S(2)}, u32[]{:S(2)}) collective-permute-start(bf16[4,4096]{1,0:T(4,128)(2,1)S(1)} %collective-permute-done.1), channel_id=1, source_target_pairs={{0,1},{1,2},{2,3},{3,4},{4,5},{5,6},{6,7},{7,8},{8,9},{9,10},{10,1... | collective-permute-start | bytes 98312 | tf_op jit(solution)/shard_map/ppermute | solution.py:21
  186.3 6.0 %collective-permute-start.9 = (bf16[4,4096]{1,0:T(4,128)(2,1)S(1)}, bf16[4,4096]{1,0:T(4,128)(2,1)S(1)}, u32[]{:S(2)}, u32[]{:S(2)}) collective-permute-start(bf16[4,4096]{1,0:T(4,128)(2,1)S(1)} %collective-permute-done.8), channel_id=1, source_target_pairs={{1,0},{2,1},{3,2},{4,3},{5,4},{6,5},{7,6},{8,7},{9,8},{10,9},{11,1... | collective-permute-start | bytes 98312 | tf_op jit(solution)/shard_map/ppermute | solution.py:27
  192.3 6.0 %collective-permute-start.3 = (bf16[4,4096]{1,0:T(4,128)(2,1)S(1)}, bf16[4,4096]{1,0:T(4,128)(2,1)S(1)}, u32[]{:S(2)}, u32[]{:S(2)}) collective-permute-start(bf16[4,4096]{1,0:T(4,128)(2,1)S(1)} %collective-permute-done.2), channel_id=1, source_target_pairs={{0,1},{1,2},{2,3},{3,4},{4,5},{5,6},{6,7},{7,8},{8,9},{9,10},{10,1... | collective-permute-start | bytes 98312 | tf_op jit(solution)/shard_map/ppermute | solution.py:21
  192.3 6.0 %collective-permute-start.10 = (bf16[4,4096]{1,0:T(4,128)(2,1)S(1)}, bf16[4,4096]{1,0:T(4,128)(2,1)S(1)}, u32[]{:S(2)}, u32[]{:S(2)}) collective-permute-start(bf16[4,4096]{1,0:T(4,128)(2,1)S(1)} %collective-permute-done.9), channel_id=1, source_target_pairs={{1,0},{2,1},{3,2},{4,3},{5,4},{6,5},{7,6},{8,7},{9,8},{10,9},{11,1... | collective-permute-start | bytes 98312 | tf_op jit(solution)/shard_map/ppermute | solution.py:27
  198.4 6.0 %collective-permute-start.4 = (bf16[4,4096]{1,0:T(4,128)(2,1)S(1)}, bf16[4,4096]{1,0:T(4,128)(2,1)S(1)}, u32[]{:S(2)}, u32[]{:S(2)}) collective-permute-start(bf16[4,4096]{1,0:T(4,128)(2,1)S(1)} %collective-permute-done.3), channel_id=1, source_target_pairs={{0,1},{1,2},{2,3},{3,4},{4,5},{5,6},{6,7},{7,8},{8,9},{9,10},{10,1... | collective-permute-start | bytes 98312 | tf_op jit(solution)/shard_map/ppermute | solution.py:21
  198.4 6.0 %collective-permute-start.11 = (bf16[4,4096]{1,0:T(4,128)(2,1)S(1)}, bf16[4,4096]{1,0:T(4,128)(2,1)S(1)}, u32[]{:S(2)}, u32[]{:S(2)}) collective-permute-start(bf16[4,4096]{1,0:T(4,128)(2,1)S(1)} %collective-permute-done.10), channel_id=1, source_target_pairs={{1,0},{2,1},{3,2},{4,3},{5,4},{6,5},{7,6},{8,7},{9,8},{10,9},{11,1... | collective-permute-start | bytes 98312 | tf_op jit(solution)/shard_map/ppermute | solution.py:27
  204.4 6.0 %collective-permute-start.5 = (bf16[4,4096]{1,0:T(4,128)(2,1)S(1)}, bf16[4,4096]{1,0:T(4,128)(2,1)S(1)}, u32[]{:S(2)}, u32[]{:S(2)}) collective-permute-start(bf16[4,4096]{1,0:T(4,128)(2,1)S(1)} %collective-permute-done.4), channel_id=1, source_target_pairs={{0,1},{1,2},{2,3},{3,4},{4,5},{5,6},{6,7},{7,8},{8,9},{9,10},{10,1... | collective-permute-start | bytes 98312 | tf_op jit(solution)/shard_map/ppermute | solution.py:21
  204.4 6.0 %collective-permute-start.12 = (bf16[4,4096]{1,0:T(4,128)(2,1)S(1)}, bf16[4,4096]{1,0:T(4,128)(2,1)S(1)}, u32[]{:S(2)}, u32[]{:S(2)}) collective-permute-start(bf16[4,4096]{1,0:T(4,128)(2,1)S(1)} %collective-permute-done.11), channel_id=1, source_target_pairs={{1,0},{2,1},{3,2},{4,3},{5,4},{6,5},{7,6},{8,7},{9,8},{10,9},{11,1... | collective-permute-start | bytes 98312 | tf_op jit(solution)/shard_map/ppermute | solution.py:27
  210.5 6.0 %collective-permute-start.6 = (bf16[4,4096]{1,0:T(4,128)(2,1)S(1)}, bf16[4,4096]{1,0:T(4,128)(2,1)S(1)}, u32[]{:S(2)}, u32[]{:S(2)}) collective-permute-start(bf16[4,4096]{1,0:T(4,128)(2,1)S(1)} %collective-permute-done.5), channel_id=1, source_target_pairs={{0,1},{1,2},{2,3},{3,4},{4,5},{5,6},{6,7},{7,8},{8,9},{9,10},{10,1... | collective-permute-start | bytes 98312 | tf_op jit(solution)/shard_map/ppermute | solution.py:21
  210.5 6.1 %collective-permute-start.13 = (bf16[4,4096]{1,0:T(4,128)(2,1)S(1)}, bf16[4,4096]{1,0:T(4,128)(2,1)S(1)}, u32[]{:S(2)}, u32[]{:S(2)}) collective-permute-start(bf16[4,4096]{1,0:T(4,128)(2,1)S(1)} %collective-permute-done.12), channel_id=1, source_target_pairs={{1,0},{2,1},{3,2},{4,3},{5,4},{6,5},{7,6},{8,7},{9,8},{10,9},{11,1... | collective-permute-start | bytes 98312 | tf_op jit(solution)/shard_map/ppermute | solution.py:27
  216.5 6.0 %collective-permute-start.7 = (bf16[4,4096]{1,0:T(4,128)(2,1)S(1)}, bf16[4,4096]{1,0:T(4,128)(2,1)S(1)}, u32[]{:S(2)}, u32[]{:S(2)}) collective-permute-start(bf16[4,4096]{1,0:T(4,128)(2,1)S(1)} %collective-permute-done.6), channel_id=1, source_target_pairs={{0,1},{1,2},{2,3},{3,4},{4,5},{5,6},{6,7},{7,8},{8,9},{9,10},{10,1... | collective-permute-start | bytes 98312 | tf_op jit(solution)/shard_map/ppermute | solution.py:21
  216.6 6.4 %collective-permute-start.14 = (bf16[4,4096]{1,0:T(4,128)(2,1)S(1)}, bf16[4,4096]{1,0:T(4,128)(2,1)S(1)}, u32[]{:S(2)}, u32[]{:S(2)}) collective-permute-start(bf16[4,4096]{1,0:T(4,128)(2,1)S(1)} %collective-permute-done.13), channel_id=1, source_target_pairs={{1,0},{2,1},{3,2},{4,3},{5,4},{6,5},{7,6},{8,7},{9,8},{10,9},{11,1... | collective-permute-start | bytes 98312 | tf_op jit(solution)/shard_map/ppermute | solution.py:27
  240.6 131.6 %all-reduce.10.cloned.1.call-start = ((), (), s32[]{:S(2)}) async-start(), calls=%async_computation.3 | async-start | bytes 2097152
Sparse Core Ops, SparseCore 0:
  12.7 56.5 all-gather.2
  74.9 92.1 all-reduce.7
  240.7 27.9 all-reduce.5
  278.8 93.3 all-reduce.9
